TPU v7x, 32 devices: a whole 2x2x4 slice. The times are simulated.
32 devices in a mesh: blk: 4 (over y, x), dp: 8 (over z, core).
Axes of the slice: x: 2, y: 2, z: 4, core: 2. Of those that a mesh axis runs over, the one named last changes fastest.
Arguments:
- embed: bfloat16 [8192, 768], P(('blk', 'dp')), may hold values from -0.23925781 to 0.23925781
- log_scale: float32 [1], replicated, may hold values from 3 to 3.7
- bias: float32 [1], replicated, may hold values from -5.5 to -3.5
- partner_count: int32 [8192], P(('blk', 'dp')), may hold values from 1 to 4, as said below
- partner_owner: int32 [8192, 4], P(('blk', 'dp')), may hold values from 0 to 31, as said below
- partner_row: int32 [8192, 4], P(('blk', 'dp')), may hold values from 0 to 255
Outputs:
- embed_grad: bfloat16 [8192, 768], P(('blk', 'dp'))
Inputs may be any that keep to these rules, and one draw needn't show every extreme that they name: `partner_count`: 4 on some row of every device. `partner_owner`: every entry names a device other than the row's own device (devices numbered index along blk times 8 plus index along dp). Among the first partner_count entries of the rows of one device, no device is named more than 34 times, and some device exactly 34 times.
All inputs are finite; a program needn't handle non-finite values.
Results may differ from a plain program's by a relative error of at most 0.0065.
Values may be sent and summed in bfloat16 or wider, within the bound.
A program may use at most 64 MiB of HBM per device.

v0:
```python
import math
import jax
import jax.numpy as jnp
from jax import lax
from jax.sharding import PartitionSpec as P


def body(embed, log_scale, bias, partner_count, partner_owner, partner_row):
    rows_here, width = embed.shape
    most = partner_owner.shape[1]
    values = embed.astype(jnp.float32)
    inv_norm = lax.rsqrt(jnp.mean(values * values, axis=1, keepdims=True) + 1e-06)
    root_width = 1.0 / math.sqrt(width)
    unit_rows = (values * inv_norm * root_width).astype(jnp.bfloat16)
    logit_scale = jnp.exp(log_scale[0])
    logit_bias = bias[0]
    my_start = lax.axis_index("blk") * rows_here
    row_ids = my_start + jnp.arange(rows_here, dtype=jnp.int32)
    group = lax.all_gather(unit_rows, "blk", axis=0, tiled=True)
    scores = lax.dot_general(
        unit_rows, group, (((1,), (1,)), ((), ())), preferred_element_type=jnp.float32
    )
    columns = jnp.arange(group.shape[0], dtype=jnp.int32)
    weights = jnp.where(
        row_ids[:, None] == columns[None, :],
        jnp.float32(0.0),
        jax.nn.sigmoid(logit_bias + logit_scale * scores),
    )
    summed = jnp.dot(weights.astype(jnp.bfloat16), group, preferred_element_type=jnp.float32)
    neg_grad = 2.0 * logit_scale * summed
    n_all = lax.axis_size(("blk", "dp"))
    capacity = -(-(rows_here * most) // (n_all - 1))
    slots_all = n_all * capacity
    owner_flat = partner_owner.reshape(-1)
    live = (jnp.arange(most, dtype=jnp.int32)[None, :] < partner_count[:, None]).reshape(-1)
    one_hot = (
        (owner_flat[:, None] == jnp.arange(n_all, dtype=jnp.int32)[None, :]) & live[:, None]
    ).astype(jnp.int32)
    earlier = jnp.cumsum(one_hot, axis=0) - one_hot
    rank_in = jnp.sum(earlier * one_hot, axis=1)
    slot_of = jnp.where(live, owner_flat * capacity + rank_in, slots_all)
    send_index = (
        jnp.zeros((slots_all,), jnp.int32).at[slot_of].set(partner_row.reshape(-1), mode="drop")
    )
    recv_index = lax.all_to_all(
        send_index.reshape(n_all, capacity), ("blk", "dp"), split_axis=0, concat_axis=0, tiled=True
    ).reshape(-1)
    safe_slot = jnp.minimum(slot_of, slots_all - 1)
    asking = jnp.broadcast_to(unit_rows[:, None, :], (rows_here, most, width)).reshape(-1, width)
    replies = unit_rows[recv_index].reshape(n_all, capacity, width)
    arrived = lax.all_to_all(
        replies, ("blk", "dp"), split_axis=0, concat_axis=0, tiled=True
    ).reshape(-1, width)
    partner = arrived[safe_slot]
    scores = jnp.einsum("nd,nd->n", asking, partner, preferred_element_type=jnp.float32)
    weight = jnp.where(live, jax.nn.sigmoid(-(logit_bias + logit_scale * scores)), jnp.float32(0.0))
    own_terms = (
        (-logit_scale * weight[:, None] * partner.astype(jnp.float32))
        .astype(jnp.bfloat16)
        .astype(jnp.float32)
    )
    back_terms = (-logit_scale * weight[:, None] * asking.astype(jnp.float32)).astype(jnp.bfloat16)
    outgoing = jnp.zeros((slots_all, width), jnp.bfloat16).at[slot_of].set(back_terms, mode="drop")
    received = lax.all_to_all(
        outgoing.reshape(n_all, capacity, width),
        ("blk", "dp"),
        split_axis=0,
        concat_axis=0,
        tiled=True,
    ).reshape(-1, width)
    incoming = jax.ops.segment_sum(received.astype(jnp.float32), recv_index, num_segments=rows_here)
    row_grad = neg_grad + jnp.sum(own_terms.reshape(rows_here, most, width), axis=1) + incoming
    inner = jnp.sum(values * row_grad, axis=1, keepdims=True)
    result = root_width * inv_norm * (row_grad - values * inv_norm * inv_norm * inner / width)
    return result.astype(jnp.bfloat16)


def solution(mesh):
    return jax.shard_map(
        body,
        mesh=mesh,
        in_specs=(
            P(("blk", "dp"), None),
            P(),
            P(),
            P(("blk", "dp")),
            P(("blk", "dp"), None),
            P(("blk", "dp"), None),
        ),
        out_specs=P(("blk", "dp"), None),
        check_vma=False,
    )
```

profile of v0, /device:TPU:0, one launch (start us, length us, event | category | flops | bytes accessed | tf_op | source)
XLA Modules:
  0.0 187.4 jit_solution(1436901027829189112)
XLA Ops:
  6.5 0.8 lt.85
  7.3 0.8 iota_compare_fusion.4
  8.1 0.8 copy.15
  9.0 0.1 eq.45
  9.2 0.1 lt.81
  9.3 0.1 lt.82
  9.5 0.7 broadcast_multiply_fusion
  10.5 9.0 %reduce-window.6 = s32[32,8,128]{2,1,0:T(8,128)S(1)} reduce-window(s32[32,8,128]{2,1,0:T(8,128)S(1)} %fusion.34, s32[]{:T(128)} %constant.21.clone.1), window={size=1x1x128 pad=0_0x0_0x127_0}, to_apply=%region_1.2 | reduce-window | flops 4161536 | bytes 262148 | tf_op jit(solution)/shard_map/reduce-window
  19.6 0.1 copy.19
  19.9 0.1 copy.14
  20.1 0.1 mul.146
  20.2 0.1 copy.21
  20.4 0.1 reshape.233
  20.6 4.3 %scatter_custom_fusion = s32[1088]{0:T(1024)S(1)} fusion(s32[1024]{0:T(1024)S(1)} %bitcast.36, s32[1024]{0:T(1024)S(1)} %reshape.233, s32[]{:T(128)} %constant.21.clone.1), kind=kCustom, calls=%fused_computation.61 | custom fusion | bytes 4356 | tf_op jit(solution)/shard_map/scatter | solution.py:43
  24.9 0.7 all_to_all.12
  25.6 7.3 %all-to-all-start = ((s32[32,1,34]{2,1,0:T(1,128)}), s32[32,1,34]{2,1,0:T(1,128)S(1)}, u32[]{:S(2)}, u32[]{:S(2)}) async-start(s32[32,1,34]{2,1,0:T(1,128)} %all_to_all.12), calls=%async_computation | async-start | bytes 32768 | tf_op jit(solution)/shard_map/all_to_all | solution.py:45
  32.9 0.2 fusion.22
  33.1 0.6 broadcast_multiply_fusion.1
  33.7 0.2 fusion.16
  33.9 6.2 %all-to-all-done = s32[32,1,34]{2,1,0:T(1,128)S(1)} async-done(((s32[32,1,34]{2,1,0:T(1,128)}), s32[32,1,34]{2,1,0:T(1,128)S(1)}, u32[]{:S(2)}, u32[]{:S(2)}) %all-to-all-start) | async-done | bytes 4384 | tf_op jit(solution)/shard_map/all_to_all | solution.py:45
  40.1 0.6 broadcast.178
  40.6 0.7 reduce.9
  41.5 4.5 %gather_fusion = bf16[1088,768]{1,0:T(8,128)(2,1)S(1)} fusion(bf16[256,768]{1,0:T(8,128)(2,1)S(1)} %fusion.16, s32[2048]{0:T(1024)S(1)} %pad_clamp_fusion), kind=kCustom, calls=%fused_computation | custom fusion | bytes 3346688 | tf_op jit(solution)/shard_map/gather | solution.py:50
  46.1 1.5 reshape.208
  47.6 3.5 %all-to-all-start.1 = ((bf16[32,34,768]{2,1,0:T(8,128)(2,1)}), bf16[32,34,768]{2,1,0:T(8,128)(2,1)}, u32[]{:S(2)}, u32[]{:S(2)}) async-start(bf16[32,34,768]{2,1,0:T(8,128)(2,1)} %reshape.208), calls=%async_computation.1 | async-start | bytes 3932160 | tf_op jit(solution)/shard_map/all_to_all | solution.py:51
  51.1 0.4 broadcast_in_dim.16
  51.5 0.4 reshape.204
  53.2 45.2 %all-to-all-done.1 = bf16[32,34,768]{2,1,0:T(8,128)(2,1)} async-done(((bf16[32,34,768]{2,1,0:T(8,128)(2,1)}), bf16[32,34,768]{2,1,0:T(8,128)(2,1)}, u32[]{:S(2)}, u32[]{:S(2)}) %all-to-all-start.1) | async-done | bytes 1671200 | tf_op jit(solution)/shard_map/all_to_all | solution.py:51
  98.4 2.5 %reshape.209 = bf16[1088,768]{1,0:T(8,128)(2,1)S(1)} reshape(bf16[32,34,768]{2,1,0:T(8,128)(2,1)} %all-to-all-done.1) | data formatting | bytes 3342336 | tf_op jit(solution)/shard_map/reshape | solution.py:53
  100.9 5.2 %gather_fusion.1 = bf16[1024,768]{1,0:T(8,128)(2,1)} fusion(bf16[1088,768]{1,0:T(8,128)(2,1)S(1)} %reshape.209, s32[1024]{0:T(1024)S(1)} %broadcast_clamp_fusion), kind=kCustom, calls=%fused_computation.1 | custom fusion | bytes 3149824 | tf_op jit(solution)/shard_map/gather | solution.py:54
  106.1 1.9 %fusion = f32[1024]{0:T(1024)S(1)} fusion(bf16[1024,768]{1,0:T(8,128)(2,1)S(1)} %reshape.204, bf16[1024,768]{1,0:T(8,128)(2,1)} %gather_fusion.1), kind=kLoop, calls=%fused_computation.7 | loop fusion | flops 3144704 | bytes 3149824 | tf_op jit(solution)/shard_map/nd,nd->n/dot_general | solution.py:55
  108.0 6.1 %scatter_custom_fusion.1 = bf16[1088,768]{1,0:T(8,128)(2,1)S(1)} fusion(s32[1024]{0:T(1024)S(1)} %bitcast.37, bf16[1024,768]{1,0:T(8,128)(2,1)S(1)} %reshape.204, f32[1024]{0:T(1024)S(1)} %select_multiply_fusion, bf16[]{:T(256)} %constant.9.clone.1), kind=kCustom, calls=%fused_computation.11 | custom fusion | flops 2359296 | bytes 3248130 | tf_op jit(solution)/shard_map/scatter | solution.py:63
  114.1 1.5 reshape.210
  115.6 2.8 %all-to-all-start.2 = ((bf16[32,34,768]{2,1,0:T(8,128)(2,1)}), bf16[32,34,768]{2,1,0:T(8,128)(2,1)S(1)}, u32[]{:S(2)}, u32[]{:S(2)}) async-start(bf16[32,34,768]{2,1,0:T(8,128)(2,1)} %reshape.210), calls=%async_computation.2 | async-start | bytes 3932160 | tf_op jit(solution)/shard_map/all_to_all | solution.py:64
  118.5 0.2 all-gather.2.cloned.1.call-start
  118.7 0.5 all-gather.2.cloned.1.call-update
  119.2 0.5 iota_add_fusion
  119.8 0.7 reshape.247
  120.5 1.5 mul.150
  121.9 2.0 %reshape.211 = f32[256,4,768]{2,1,0:T(4,128)} reshape(bf16[1024,768]{1,0:T(8,128)(2,1)S(1)} %copy-done.2) | data formatting | bytes 4718592 | tf_op jit(solution)/shard_map/convert_element_type | solution.py:58
  124.0 4.8 %convert_reduce_fusion = f32[256,768]{1,0:T(8,128)} fusion(f32[256,4,768]{2,1,0:T(4,128)} %reshape.211, f32[256,4]{1,0:T(8,128)} %mul.150), kind=kLoop, calls=%fused_computation.9 | loop fusion | flops 2949120 | bytes 3936256 | tf_op jit(solution)/shard_map/reduce_sum | solution.py:72
  128.8 32.2 %all-gather.2.cloned.1.call-done = bf16[1024,768]{1,0:T(8,128)(2,1)} async-done(((bf16[256,768]{1,0:T(8,128)(2,1)}), bf16[1024,768]{1,0:T(8,128)(2,1)}) %all-gather.2.cloned.1.call-update) | async-done | bytes 1572880 | tf_op jit(solution)/shard_map/all_gather | solution.py:19
  161.0 3.3 %fusion.10 = f32[256,768]{1,0:T(8,128)S(1)} fusion(f32[256,768]{1,0:T(8,128)} %convert_reduce_fusion, bf16[1024,768]{1,0:T(8,128)(2,1)} %all-gather.2.cloned.1.call-done, bf16[256,768]{1,0:T(8,128)(2,1)S(1)} %copy-done.1, f32[]{:T(128)} %bitcast, f32[]{:T(128)} %bitcast.28, s32[256]{0:T(256)S(1)} %copy-done.11, f32[]{:T(128)S(6)} %mul_shard_map.3), kind=kOutput, calls=%fused_computation.20 | convolution fusion | flops 807796736 | bytes 3539980 | tf_op jit(solution)/shard_map/dot_general | solution.py:29
  164.3 1.5 all-to-all-done.2
  165.9 1.9 %reshape.249 = f32[1088,768]{1,0:T(8,128)} reshape(bf16[32,34,768]{2,1,0:T(8,128)(2,1)S(1)} %all-to-all-done.2) | data formatting | bytes 5013504 | tf_op jit(solution)/shard_map/convert_element_type | solution.py:71
  167.8 11.6 %scatter_fusion = f32[256,768]{1,0:T(8,128)S(1)} fusion(f32[256,768]{1,0:T(8,128)S(1)} %fusion.10, s32[1088]{0:T(1024)S(1)} %copy-done.6, f32[1088,768]{1,0:T(8,128)} %reshape.249), kind=kCustom, calls=%fused_computation.4 | custom fusion | flops 835584 | bytes 10031360 | tf_op jit(solution)/shard_map/scatter-add | solution.py:71
  179.4 0.2 fusion.23
  179.5 1.0 fusion.21
  (44 shorter events, 1.0 us)
Async XLA Ops:
  6.5 13.7 %copy-start.9 = (s32[256,4]{0,1:T(4,128)S(1)}, s32[256,4]{0,1:T(4,128)}, u32[]{:S(2)}) copy-start(s32[256,4]{0,1:T(4,128)} %param.11) | copy-start | bytes 12292
  6.5 26.4 %copy-start.3 = (bf16[256,768]{1,0:T(8,128)(2,1)S(1)}, bf16[256,768]{1,0:T(8,128)(2,1)}, u32[]{:S(2)}) copy-start(bf16[256,768]{1,0:T(8,128)(2,1)} %param.6) | copy-start | bytes 1179652
  25.6 14.4 %all-to-all-start = ((s32[32,1,34]{2,1,0:T(1,128)}), s32[32,1,34]{2,1,0:T(1,128)S(1)}, u32[]{:S(2)}, u32[]{:S(2)}) async-start(s32[32,1,34]{2,1,0:T(1,128)} %all_to_all.12), calls=%async_computation | async-start | bytes 32768 | tf_op jit(solution)/shard_map/all_to_all | solution.py:45
  33.7 12.4 %copy-start.7 = (f32[256]{0:T(256)}, f32[256]{0:T(256)S(1)}, u32[]{:S(2)}) copy-start(f32[256]{0:T(256)S(1)} %get-tuple-element.8) | copy-start | bytes 3076
  33.8 17.2 %copy-start = (bf16[256,768]{1,0:T(8,128)(2,1)}, bf16[256,768]{1,0:T(8,128)(2,1)S(1)}, u32[]{:S(2)}) copy-start(bf16[256,768]{1,0:T(8,128)(2,1)S(1)} %fusion.16) | copy-start | bytes 1179652
  47.6 50.8 %all-to-all-start.1 = ((bf16[32,34,768]{2,1,0:T(8,128)(2,1)}), bf16[32,34,768]{2,1,0:T(8,128)(2,1)}, u32[]{:S(2)}, u32[]{:S(2)}) async-start(bf16[32,34,768]{2,1,0:T(8,128)(2,1)} %reshape.208), calls=%async_computation.1 | async-start | bytes 3932160 | tf_op jit(solution)/shard_map/all_to_all | solution.py:51
  108.0 6.1 %copy-start.5 = (f32[1024]{0:T(1024)}, f32[1024]{0:T(1024)S(1)}, u32[]{:S(2)}) copy-start(f32[1024]{0:T(1024)S(1)} %select_multiply_fusion) | copy-start | bytes 12292
  115.6 6.3 %copy-start.2 = (bf16[1024,768]{1,0:T(8,128)(2,1)S(1)}, bf16[1024,768]{1,0:T(8,128)(2,1)}, u32[]{:S(2)}) copy-start(bf16[1024,768]{1,0:T(8,128)(2,1)} %gather_fusion.1) | copy-start | bytes 4718596
  115.6 50.2 %all-to-all-start.2 = ((bf16[32,34,768]{2,1,0:T(8,128)(2,1)}), bf16[32,34,768]{2,1,0:T(8,128)(2,1)S(1)}, u32[]{:S(2)}, u32[]{:S(2)}) async-start(bf16[32,34,768]{2,1,0:T(8,128)(2,1)} %reshape.210), calls=%async_computation.2 | async-start | bytes 3932160 | tf_op jit(solution)/shard_map/all_to_all | solution.py:64
  118.5 42.5 %all-gather.2.cloned.1.call-start = ((), (), s32[]{:S(2)}) async-start(), calls=%async_computation.3 | async-start | bytes 1966080 | tf_op jit(solution)/shard_map/all_gather | solution.py:19
  124.0 37.0 %copy-start.1 = (bf16[256,768]{1,0:T(8,128)(2,1)S(1)}, bf16[256,768]{1,0:T(8,128)(2,1)}, u32[]{:S(2)}) copy-start(bf16[256,768]{1,0:T(8,128)(2,1)} %copy-done) | copy-start | bytes 1179652
  124.0 37.0 %copy-start.11 = (s32[256]{0:T(256)S(1)}, s32[256]{0:T(256)}, u32[]{:S(2)}) copy-start(s32[256]{0:T(256)} %iota_add_fusion) | copy-start | bytes 3076
  164.3 3.4 %copy-start.6 = (s32[1088]{0:T(1024)S(1)}, s32[1088]{0:T(1024)}, u32[]{:S(2)}) copy-start(s32[1088]{0:T(1024)} %reshape.247) | copy-start | bytes 13060
  167.8 11.6 %copy-start.4 = (bf16[256,768]{1,0:T(8,128)(2,1)S(1)}, bf16[256,768]{1,0:T(8,128)(2,1)}, u32[]{:S(2)}) copy-start(bf16[256,768]{1,0:T(8,128)(2,1)} %param.6) | copy-start | bytes 1179652
  167.8 11.8 %copy-start.8 = (f32[256]{0:T(256)S(1)}, f32[256]{0:T(256)}, u32[]{:S(2)}) copy-start(f32[256]{0:T(256)} %copy-done.7) | copy-start | bytes 3076
  167.8 11.8 %copy-start.10 = (f32[256]{0:T(256)S(1)}, f32[256]{0:T(256)}, u32[]{:S(2)}) copy-start(f32[256]{0:T(256)} %get-tuple-element.7) | copy-start | bytes 3076
Sparse Core Ops, SparseCore 0:
  121.2 39.7 all-gather.1
where the time goes:
time: 188 us; the launch traced here: 187 us
  waiting for transfers between devices  85.6 us (46%)
  other arithmetic  38.4 us (20%)
  local copies, waits for them, and re-layouts  31.1 us (17%)
  between operations  15.1 us (8%)
  starting transfers between devices  13.8 us (7%)
  matrix products  3.34 us (2%)
    all_to_all x1, waiting for transfers between devices, body(): lax.all_to_all(replies, ('blk', 'dp'), split_axis=0, concat_axis=0, tiled...  45.2 us
    all_gather x1, waiting for transfers between devices, body(): group = lax.all_gather(unit_rows, 'blk', axis=0, tiled=True)  32.2 us
    scatter-add x1, other arithmetic, body(): jax.ops.segment_sum(received.astype(jnp.float32), recv_index, num_segment...  11.6 us
    another operation x3, other arithmetic  9.15 us
    all_to_all x1, starting transfers between devices, body(): lax.all_to_all(send_index.reshape(n_all, capacity), ('blk', 'dp'), split_...  7.3 us
    all_to_all x1, waiting for transfers between devices, body(): lax.all_to_all(send_index.reshape(n_all, capacity), ('blk', 'dp'), split_...  6.2 us
    scatter x1, other arithmetic, body(): jnp.zeros((slots_all, width), jnp.bfloat16).at[slot_of]  6.08 us
    gather x1, local copies, waits for them, and re-layouts, body(): partner = arrived[safe_slot]  5.21 us
  transfers between devices with their start and end apart: 4, of which 4 were waited for; matrix products, arithmetic and copies ran while one was open for 8% of the time, Pallas kernels for 0%

commit v1 on v0

--- a/solution.py
+++ b/solution.py
@@ -16,7 +16,24 @@
     logit_bias = bias[0]
     my_start = lax.axis_index("blk") * rows_here
     row_ids = my_start + jnp.arange(rows_here, dtype=jnp.int32)
-    group = lax.all_gather(unit_rows, "blk", axis=0, tiled=True)
+    a_next = lax.axis_size("blk")
+    inbox = []
+    w2, part_now, z1 = (a_next, lax.axis_index("blk"), unit_rows.shape[0])
+    for m in range(w2):
+        inbox.append((m, (m + 1) % w2))
+    pieces_in = []
+    for m in range(w2):
+        pieces_in.append((m, (m - 1) % w2))
+    group = jnp.zeros((*unit_rows.shape[:0], w2 * z1, *unit_rows.shape[1:]), unit_rows.dtype)
+    group = lax.dynamic_update_slice_in_dim(group, unit_rows, part_now * z1, axis=0)
+    all_values = b_next = unit_rows
+    o_now = w2 // 2
+    for s in range(1, o_now + 1):
+        all_values = lax.ppermute(all_values, "blk", inbox)
+        group = lax.dynamic_update_slice_in_dim(group, all_values, (part_now - s) % w2 * z1, axis=0)
+        if s < w2 - o_now:
+            b_next = lax.ppermute(b_next, "blk", pieces_in)
+            group = lax.dynamic_update_slice_in_dim(group, b_next, (part_now + s) % w2 * z1, axis=0)
     scores = lax.dot_general(
         unit_rows, group, (((1,), (1,)), ((), ())), preferred_element_type=jnp.float32
     )

time: 188 us -> 195 us (1.037)
  between operations: 15.1 us -> 1.64 us
  waiting for transfers between devices: 85.6 us -> 95 us
  local copies, waits for them, and re-layouts: 31.1 us -> 38.6 us
  starting transfers between devices: 13.8 us -> 17.2 us
    ppermute x0 -> x3, waiting for transfers between devices: none -> 46.1 us  [the longest x2 36.1 us: body(): all_values = lax.ppermute(all_values, 'blk', inbox)]
    all_gather x1 -> x0, waiting for transfers between devices: 32.2 us -> none  [body(): group = lax.all_gather(unit_rows, 'blk', axis=0, tiled=True)]
    dynamic_update_slice x0 -> x3, local copies, waits for them, and re-layouts: none -> 3.34 us  [the longest x1 1.77 us: body(): lax.dynamic_update_slice_in_dim(group, b_next, (part_now + s) % w2 * z1,...]
    ppermute x0 -> x3, starting transfers between devices: none -> 2.98 us  [the longest x2 1.63 us: body(): all_values = lax.ppermute(all_values, 'blk', inbox)]
  transfers between devices with their start and end apart: 4 -> 6, of which waited for: 4 -> 5; matrix products, arithmetic and copies ran while one was open for 8% -> 9% of each run, Pallas kernels for 0% -> 0%
where the time goes in v1:
time: 195 us; the launch traced here: 194 us
  waiting for transfers between devices  95 us (49%)
  local copies, waits for them, and re-layouts  38.6 us (20%)
  other arithmetic  38.5 us (20%)
  starting transfers between devices  17.2 us (9%)
  matrix products  3.08 us (2%)
    all_to_all x1, waiting for transfers between devices, body(): lax.all_to_all(replies, ('blk', 'dp'), split_axis=0, concat_axis=0, tiled...  44.2 us
    ppermute x2, waiting for transfers between devices, body(): all_values = lax.ppermute(all_values, 'blk', inbox)  36.1 us
    scatter-add x1, other arithmetic, body(): jax.ops.segment_sum(received.astype(jnp.float32), recv_index, num_segment...  11.6 us
    ppermute x1, waiting for transfers between devices, body(): b_next = lax.ppermute(b_next, 'blk', pieces_in)  9.96 us
    another operation x3, other arithmetic  9.15 us
    all_to_all x1, starting transfers between devices, body(): lax.all_to_all(send_index.reshape(n_all, capacity), ('blk', 'dp'), split_...  7.3 us
    scatter x1, other arithmetic, body(): jnp.zeros((slots_all, width), jnp.bfloat16).at[slot_of]  6.92 us
    gather x1, local copies, waits for them, and re-layouts, body(): partner = arrived[safe_slot]  5.27 us
  transfers between devices with their start and end apart: 6, of which 5 were waited for; matrix products, arithmetic and copies ran while one was open for 9% of the time, Pallas kernels for 0%

profile of v1, /device:TPU:0, one launch (start us, length us, event | category | flops | bytes accessed | tf_op | source)
XLA Modules:
  0.0 194.0 jit_solution(17585222091225125952)
XLA Ops:
  0.0 0.8 lt.118
  0.8 0.8 iota_compare_fusion.4
  1.6 0.8 copy.15
  2.7 0.1 lt.114
  2.8 0.1 lt.115
  2.9 0.7 broadcast_multiply_fusion
  3.9 9.0 %reduce-window.6 = s32[32,8,128]{2,1,0:T(8,128)S(1)} reduce-window(s32[32,8,128]{2,1,0:T(8,128)S(1)} %fusion.34, s32[]{:T(128)} %constant.63.clone.1), window={size=1x1x128 pad=0_0x0_0x127_0}, to_apply=%region_1.2 | reduce-window | flops 4161536 | bytes 262148 | tf_op jit(solution)/shard_map/reduce-window
  13.1 0.1 copy.19
  13.4 0.1 copy.14
  13.6 0.1 mul.159
  13.7 0.1 copy.21
  14.0 4.3 %scatter_custom_fusion = s32[1088]{0:T(1024)S(1)} fusion(s32[1024]{0:T(1024)S(1)} %bitcast.36, s32[1024]{0:T(1024)S(1)} %reshape.233, s32[]{:T(128)} %constant.63.clone.1), kind=kCustom, calls=%fused_computation.61 | custom fusion | bytes 4356 | tf_op jit(solution)/shard_map/scatter | solution.py:60
  18.4 0.7 all_to_all.12
  19.1 7.3 %all-to-all-start = ((s32[32,1,34]{2,1,0:T(1,128)}), s32[32,1,34]{2,1,0:T(1,128)S(1)}, u32[]{:S(2)}, u32[]{:S(2)}) async-start(s32[32,1,34]{2,1,0:T(1,128)} %all_to_all.12), calls=%async_computation | async-start | bytes 32768 | tf_op jit(solution)/shard_map/all_to_all | solution.py:62
  26.4 0.2 fusion.22
  26.6 1.3 broadcast_in_dim.18
  27.8 0.9 constant_dynamic-update-slice_fusion.3
  28.7 4.7 %all-to-all-done = s32[32,1,34]{2,1,0:T(1,128)S(1)} async-done(((s32[32,1,34]{2,1,0:T(1,128)}), s32[32,1,34]{2,1,0:T(1,128)S(1)}, u32[]{:S(2)}, u32[]{:S(2)}) %all-to-all-start) | async-done | bytes 4384 | tf_op jit(solution)/shard_map/all_to_all | solution.py:62
  33.5 0.5 broadcast.181
  34.0 0.7 reduce.9
  34.8 4.5 %gather_fusion = bf16[1088,768]{1,0:T(8,128)(2,1)S(1)} fusion(bf16[256,768]{1,0:T(8,128)(2,1)S(1)} %get-tuple-element.6, s32[2048]{0:T(1024)S(1)} %pad_clamp_fusion), kind=kCustom, calls=%fused_computation | custom fusion | bytes 3346688 | tf_op jit(solution)/shard_map/gather | solution.py:67
  39.3 1.6 reshape.208
  40.9 3.5 %all-to-all-start.1 = ((bf16[32,34,768]{2,1,0:T(8,128)(2,1)}), bf16[32,34,768]{2,1,0:T(8,128)(2,1)}, u32[]{:S(2)}, u32[]{:S(2)}) async-start(bf16[32,34,768]{2,1,0:T(8,128)(2,1)} %reshape.208), calls=%async_computation.1 | async-start | bytes 3932160 | tf_op jit(solution)/shard_map/all_to_all | solution.py:68
  44.4 0.4 broadcast_in_dim.19
  44.8 1.4 reshape.204
  47.5 44.2 %all-to-all-done.1 = bf16[32,34,768]{2,1,0:T(8,128)(2,1)} async-done(((bf16[32,34,768]{2,1,0:T(8,128)(2,1)}), bf16[32,34,768]{2,1,0:T(8,128)(2,1)}, u32[]{:S(2)}, u32[]{:S(2)}) %all-to-all-start.1) | async-done | bytes 1671200 | tf_op jit(solution)/shard_map/all_to_all | solution.py:68
  91.7 2.5 %reshape.209 = bf16[1088,768]{1,0:T(8,128)(2,1)S(1)} reshape(bf16[32,34,768]{2,1,0:T(8,128)(2,1)} %all-to-all-done.1) | data formatting | bytes 3342336 | tf_op jit(solution)/shard_map/reshape | solution.py:70
  94.2 5.3 %gather_fusion.1 = bf16[1024,768]{1,0:T(8,128)(2,1)} fusion(bf16[1088,768]{1,0:T(8,128)(2,1)S(1)} %reshape.209, s32[1024]{0:T(1024)S(1)} %broadcast_clamp_fusion), kind=kCustom, calls=%fused_computation.1 | custom fusion | bytes 3149824 | tf_op jit(solution)/shard_map/gather | solution.py:71
  99.5 2.5 %fusion = f32[1024]{0:T(1024)S(1)} fusion(bf16[1024,768]{1,0:T(8,128)(2,1)} %reshape.204, bf16[1024,768]{1,0:T(8,128)(2,1)} %gather_fusion.1), kind=kLoop, calls=%fused_computation.7 | loop fusion | flops 3144704 | bytes 3149824 | tf_op jit(solution)/shard_map/nd,nd->n/dot_general | solution.py:72
  102.0 6.9 %scatter_custom_fusion.1 = bf16[1088,768]{1,0:T(8,128)(2,1)} fusion(s32[1024]{0:T(1024)S(1)} %bitcast.37, bf16[1024,768]{1,0:T(8,128)(2,1)S(1)} %copy-done, f32[1024]{0:T(1024)S(1)} %select_multiply_fusion, bf16[]{:T(256)} %constant.62.clone.1), kind=kCustom, calls=%fused_computation.11 | custom fusion | flops 2359296 | bytes 3248130 | tf_op jit(solution)/shard_map/scatter | solution.py:80
  108.9 3.5 %reshape.210 = bf16[32,34,768]{2,1,0:T(8,128)(2,1)} reshape(bf16[1088,768]{1,0:T(8,128)(2,1)} %scatter_custom_fusion.1) | data formatting | bytes 3342336 | tf_op jit(solution)/shard_map/reshape | solution.py:82
  112.4 3.5 %all-to-all-start.2 = ((bf16[32,34,768]{2,1,0:T(8,128)(2,1)}), bf16[32,34,768]{2,1,0:T(8,128)(2,1)}, u32[]{:S(2)}, u32[]{:S(2)}) async-start(bf16[32,34,768]{2,1,0:T(8,128)(2,1)} %reshape.210), calls=%async_computation.2 | async-start | bytes 3932160 | tf_op jit(solution)/shard_map/all_to_all | solution.py:81
  115.9 1.6 collective-permute-start
  117.5 1.4 collective-permute-start.1
  118.8 26.8 %collective-permute-done = bf16[256,768]{1,0:T(8,128)(2,1)S(1)} collective-permute-done((bf16[256,768]{1,0:T(8,128)(2,1)S(1)}, bf16[256,768]{1,0:T(8,128)(2,1)S(1)}, u32[]{:S(2)}, u32[]{:S(2)}) %collective-permute-start) | collective-permute-done | bytes 393248 | tf_op jit(solution)/shard_map/ppermute | solution.py:32
  145.8 0.8 constant_dynamic-update-slice_fusion.2
  146.6 10.0 %collective-permute-done.1 = bf16[256,768]{1,0:T(8,128)(2,1)} collective-permute-done((bf16[256,768]{1,0:T(8,128)(2,1)S(1)}, bf16[256,768]{1,0:T(8,128)(2,1)}, u32[]{:S(2)}, u32[]{:S(2)}) %collective-permute-start.1) | collective-permute-done | bytes 393248 | tf_op jit(solution)/shard_map/ppermute | solution.py:35
  156.5 1.8 constant_dynamic-update-slice_fusion.1
  158.3 9.3 %collective-permute-done.2 = bf16[256,768]{1,0:T(8,128)(2,1)S(1)} collective-permute-done((bf16[256,768]{1,0:T(8,128)(2,1)S(1)}, bf16[256,768]{1,0:T(8,128)(2,1)S(1)}, u32[]{:S(2)}, u32[]{:S(2)}) %collective-permute-start.2) | collective-permute-done | bytes 393248 | tf_op jit(solution)/shard_map/ppermute | solution.py:32
  167.6 0.8 constant_dynamic-update-slice_fusion
  168.4 0.1 mul.163
  168.5 2.1 %reshape.211 = f32[256,4,768]{2,1,0:T(4,128)} reshape(bf16[1024,768]{1,0:T(8,128)(2,1)S(1)} %copy-done.1) | data formatting | bytes 4718592 | tf_op jit(solution)/shard_map/convert_element_type | solution.py:75
  170.6 3.8 %convert_reduce_fusion = f32[256,768]{1,0:T(8,128)S(1)} fusion(f32[256,4,768]{2,1,0:T(4,128)} %reshape.211, f32[256,4]{1,0:T(8,128)S(1)} %mul.163), kind=kLoop, calls=%fused_computation.9 | loop fusion | flops 2949120 | bytes 3936256 | tf_op jit(solution)/shard_map/reduce_sum | solution.py:89
  174.4 3.1 %fusion.10 = f32[256,768]{1,0:T(8,128)S(1)} fusion(f32[256,768]{1,0:T(8,128)S(1)} %convert_reduce_fusion, bf16[1024,768]{1,0:T(8,128)(2,1)} %constant_dynamic-update-slice_fusion, bf16[256,768]{1,0:T(8,128)(2,1)S(1)} %get-tuple-element.6, f32[]{:T(128)} %bitcast, f32[]{:T(128)} %bitcast.28, s32[256]{0:T(256)S(1)} %iota_add_fusion, f32[]{:T(128)S(6)} %mul_shard_map.3), kind=kOutput, calls=%fused_computation.20 | convolution fusion | flops 807796736 | bytes 3539980 | tf_op jit(solution)/shard_map/dot_general | solution.py:46
  177.5 3.7 %reshape.249 = f32[1088,768]{1,0:T(8,128)} reshape(bf16[32,34,768]{2,1,0:T(8,128)(2,1)} %all-to-all-done.2) | data formatting | bytes 5013504 | tf_op jit(solution)/shard_map/convert_element_type | solution.py:88
  181.3 11.6 %scatter_fusion = f32[256,768]{1,0:T(8,128)S(1)} fusion(f32[256,768]{1,0:T(8,128)S(1)} %fusion.10, s32[1088]{0:T(1024)S(1)} %reshape.247, f32[1088,768]{1,0:T(8,128)} %reshape.249), kind=kCustom, calls=%fused_computation.4 | custom fusion | flops 835584 | bytes 10031360 | tf_op jit(solution)/shard_map/scatter-add | solution.py:88
  192.8 0.2 fusion.23
  193.0 1.0 fusion.21
  (35 shorter events, 1.3 us)
Async XLA Ops:
  0.0 13.7 %copy-start.3 = (s32[256,4]{0,1:T(4,128)S(1)}, s32[256,4]{0,1:T(4,128)}, u32[]{:S(2)}) copy-start(s32[256,4]{0,1:T(4,128)} %param.11) | copy-start | bytes 12292
  0.0 26.4 %copy-start.2 = (bf16[256,768]{1,0:T(8,128)(2,1)S(1)}, bf16[256,768]{1,0:T(8,128)(2,1)}, u32[]{:S(2)}) copy-start(bf16[256,768]{1,0:T(8,128)(2,1)} %param.6) | copy-start | bytes 1179652
  19.1 14.4 %all-to-all-start = ((s32[32,1,34]{2,1,0:T(1,128)}), s32[32,1,34]{2,1,0:T(1,128)S(1)}, u32[]{:S(2)}, u32[]{:S(2)}) async-start(s32[32,1,34]{2,1,0:T(1,128)} %all_to_all.12), calls=%async_computation | async-start | bytes 32768 | tf_op jit(solution)/shard_map/all_to_all | solution.py:62
  40.9 50.8 %all-to-all-start.1 = ((bf16[32,34,768]{2,1,0:T(8,128)(2,1)}), bf16[32,34,768]{2,1,0:T(8,128)(2,1)}, u32[]{:S(2)}, u32[]{:S(2)}) async-start(bf16[32,34,768]{2,1,0:T(8,128)(2,1)} %reshape.208), calls=%async_computation.1 | async-start | bytes 3932160 | tf_op jit(solution)/shard_map/all_to_all | solution.py:68
  99.5 2.5 %copy-start = (bf16[1024,768]{1,0:T(8,128)(2,1)S(1)}, bf16[1024,768]{1,0:T(8,128)(2,1)}, u32[]{:S(2)}) copy-start(bf16[1024,768]{1,0:T(8,128)(2,1)} %reshape.204) | copy-start | bytes 4718596
  112.4 65.1 %all-to-all-start.2 = ((bf16[32,34,768]{2,1,0:T(8,128)(2,1)}), bf16[32,34,768]{2,1,0:T(8,128)(2,1)}, u32[]{:S(2)}, u32[]{:S(2)}) async-start(bf16[32,34,768]{2,1,0:T(8,128)(2,1)} %reshape.210), calls=%async_computation.2 | async-start | bytes 3932160 | tf_op jit(solution)/shard_map/all_to_all | solution.py:81
  115.8 52.7 %copy-start.1 = (bf16[1024,768]{1,0:T(8,128)(2,1)S(1)}, bf16[1024,768]{1,0:T(8,128)(2,1)}, u32[]{:S(2)}) copy-start(bf16[1024,768]{1,0:T(8,128)(2,1)} %gather_fusion.1) | copy-start | bytes 4718596
  115.9 29.8 %collective-permute-start = (bf16[256,768]{1,0:T(8,128)(2,1)S(1)}, bf16[256,768]{1,0:T(8,128)(2,1)S(1)}, u32[]{:S(2)}, u32[]{:S(2)}) collective-permute-start(bf16[256,768]{1,0:T(8,128)(2,1)S(1)} %get-tuple-element.6), channel_id=1, source_target_pairs={{0,8},{8,16},{16,24},{24,0},{1,9},{9,17},{17,25},{25,1},{2,10},{10... | collective-permute-start | bytes 1179656 | tf_op jit(solution)/shard_map/ppermute | solution.py:32
  117.5 39.0 %collective-permute-start.1 = (bf16[256,768]{1,0:T(8,128)(2,1)S(1)}, bf16[256,768]{1,0:T(8,128)(2,1)}, u32[]{:S(2)}, u32[]{:S(2)}) collective-permute-start(bf16[256,768]{1,0:T(8,128)(2,1)S(1)} %get-tuple-element.6), channel_id=1, source_target_pairs={{0,24},{8,0},{16,8},{24,16},{1,25},{9,1},{17,9},{25,17},{2,26},{10... | collective-permute-start | bytes 1179656 | tf_op jit(solution)/shard_map/ppermute | solution.py:35
  145.6 22.0 %collective-permute-start.2 = (bf16[256,768]{1,0:T(8,128)(2,1)S(1)}, bf16[256,768]{1,0:T(8,128)(2,1)S(1)}, u32[]{:S(2)}, u32[]{:S(2)}) collective-permute-start(bf16[256,768]{1,0:T(8,128)(2,1)S(1)} %collective-permute-done), channel_id=1, source_target_pairs={{0,8},{8,16},{16,24},{24,0},{1,9},{9,17},{17,25},{25,1},{2,10},{10... | collective-permute-start | bytes 1179656 | tf_op jit(solution)/shard_map/ppermute | solution.py:32
